TPU v7x, 32 devices: a whole 2x2x4 slice. The times are simulated.
32 devices in a mesh: node: 8 (over z, core), edge: 4 (over y, x).
Axes of the slice: x: 2, y: 2, z: 4, core: 2. Of those that a mesh axis runs over, the one named last changes fastest.
Arguments:
- node_feats: bfloat16 [4096, 512], P(('node', 'edge')), may hold values from -40 to 40
- members: int32 [8, 4, 3072], P('node', None, 'edge'), may hold values from 0 to 511, as said below
- incidence_mask: int32 [8, 4, 3072], P('node', None, 'edge'), may hold values from 0 to 1
- degrees: int32 [3072], P(('edge', 'node')), may hold values from 0 to 32, as said below
- w_query: bfloat16 [512, 512], replicated, may hold values from -1 to 1
- w_key: bfloat16 [512, 512], replicated, may hold values from -1 to 1
- w_value: bfloat16 [512, 512], replicated, may hold values from -0.25 to 0.25
- w_out: bfloat16 [512, 512], replicated, may hold values from -0.5 to 0.5
Outputs:
- mixed: bfloat16 [3072, 512], P(('edge', 'node'))
Inputs may be any that keep to these rules, and one draw needn't show every extreme that they name: `members`: node index within the partition; only slots whose incidence_mask is 1 count. degrees[h] is the number of slots of hyperedge h over all partitions whose incidence_mask is 1; some hyperedge has every slot of every partition filled, and some hyperedge has none.
All inputs are finite; a program needn't handle non-finite values.
Results may differ from a plain program's by a relative error of at most 0.012.
Values may be sent and summed in bfloat16 or wider, within the bound.
No kernel may reach another device: no remote copies, remote signals or barrier semaphores. Data moves between devices by JAX's collectives and lax.ppermute only.
A program may use at most 64 MiB of HBM per device.

v0:
```python
import math
import jax
import jax.numpy as jnp
from jax import lax
from jax.sharding import PartitionSpec as P


def feature_map(values):
    return jax.nn.elu(values) + 1.0


def body(node_feats, members, incidence_mask, degrees, w_query, w_key, w_value, w_out):
    gathered = lax.all_gather(node_feats, "edge", axis=0, tiled=True)
    node_count = gathered.shape[0]
    width = gathered.shape[1]
    member_slots = members[0]
    slot_valid = incidence_mask[0]
    owned = degrees.shape[0]
    node_columns = lax.broadcasted_iota(jnp.int32, (1, node_count), 1)

    def block_term(first_row, block_size):
        slot_index = lax.dynamic_slice_in_dim(member_slots, first_row, block_size, 1)
        slot_keep = lax.dynamic_slice_in_dim(slot_valid, first_row, block_size, 1)
        counts = jnp.zeros((block_size, node_count), jnp.bfloat16)
        for slot in range(slot_index.shape[0]):
            hits = jnp.where(slot_index[slot][:, None] == node_columns, slot_keep[slot][:, None], 0)
            counts = counts + hits.astype(jnp.bfloat16)
        return jnp.dot(counts, gathered, preferred_element_type=jnp.float32)

    block_size = math.gcd(lax.axis_size("node") * owned, 512)
    block_total = lax.axis_size("node") * owned // block_size

    def block_rows(block):
        return block_term(block * block_size, block_size)

    stacked = lax.map(block_rows, jnp.arange(block_total, dtype=jnp.int32))
    hedge_sum = lax.psum_scatter(
        stacked.reshape(lax.axis_size("node") * owned, width).astype(jnp.bfloat16),
        "node",
        scatter_dimension=0,
        tiled=True,
    ).astype(jnp.float32)
    scale = jnp.maximum(degrees, 1).astype(jnp.float32)
    hedge = (hedge_sum / scale[:, None]).astype(jnp.bfloat16)
    query_proj = jnp.dot(hedge, w_query, preferred_element_type=jnp.float32)
    key_proj = jnp.dot(hedge, w_key, preferred_element_type=jnp.float32)
    value_proj = jnp.dot(hedge, w_value, preferred_element_type=jnp.float32)
    query_feats = feature_map(query_proj).astype(jnp.bfloat16)
    key_feats = feature_map(key_proj).astype(jnp.bfloat16)
    value_rows = value_proj.astype(jnp.bfloat16)
    gram_local = lax.dot_general(
        key_feats, value_rows, (((0,), (0,)), ((), ())), preferred_element_type=jnp.float32
    )
    key_local = jnp.sum(key_feats.astype(jnp.float32), axis=0)
    query_wide = query_feats.astype(jnp.float32)
    gram_whole, key_whole = lax.psum((gram_local, key_local), ("node", "edge"))
    numer = jnp.dot(query_wide, gram_whole, precision=lax.Precision.HIGHEST)
    denom = jnp.dot(query_wide, key_whole, precision=lax.Precision.HIGHEST)
    attended = (numer / denom[:, None]).astype(jnp.bfloat16)
    mixed = hedge.astype(jnp.float32) + jnp.dot(attended, w_out, preferred_element_type=jnp.float32)
    return mixed.astype(jnp.bfloat16)


def solution(mesh):
    placed = (
        P(("node", "edge"), None),
        P("node", None, "edge"),
        P("node", None, "edge"),
        P(("edge", "node")),
        P(),
        P(),
        P(),
        P(),
    )
    return jax.shard_map(
        body, mesh=mesh, in_specs=placed, out_specs=P(("edge", "node"), None), check_vma=False
    )
```

profile of v0, /device:TPU:0, one launch (start us, length us, event | category | flops | bytes accessed | tf_op | source)
XLA Modules:
  0.0 203.7 jit_solution(6001227106174851907)
XLA Ops:
  6.5 0.0 copy-start
  6.5 0.0 reduce-scatter.2.cloned.1.call-start
  6.5 12.0 %all_gather.3 = bf16[512,512]{1,0:T(8,128)(2,1)S(1)} all-gather(bf16[128,512]{1,0:T(8,128)(2,1)} %param.10), channel_id=1, replica_groups=mesh['node'=8,'edge'=4] {'edge'}, dimensions={0}, use_global_device_ids=true | all-gather | bytes 655360 | tf_op jit(solution)/shard_map/all_gather | solution.py:13
  18.5 8.1 %while.12 = (s32[]{:T(128)}, bf16[3,256,512]{2,1,0:T(8,128)(2,1)S(1)}, s32[3]{0:T(128)S(1)}, s32[4,768]{1,0:T(4,128)}, s32[4,768]{1,0:T(4,128)}, /*index=5*/bf16...) while((s32[]{:T(128)}, ...), condition=%wide.region_1.2_spmd.clone.clone, body=%wide.region_0.1_spmd.clone.clone.sunk | while | flops 136839168 | bytes 1073399 | solution.py:36
  18.5 0.6 dynamic_slice.17
  19.8 0.9 constant_dynamic-slice_fusion.3
  20.7 0.5 fusion.46
  21.3 0.6 dynamic_slice.17
  22.5 0.9 constant_dynamic-slice_fusion.3
  23.4 0.5 fusion.46
  24.0 0.6 dynamic_slice.17
  25.2 0.9 constant_dynamic-slice_fusion.3
  26.1 0.5 fusion.46
  26.7 0.0 copy-start.1
  26.7 0.0 copy-start.3
  26.7 0.0 copy-start.6
  26.7 0.9 copy-done.1
  27.6 0.0 reduce-scatter.2.cloned.1.call-update
  27.6 0.0 all-reduce.2.cloned.1.call-start
  27.6 0.0 copy-done.6
  27.7 32.2 %reduce-scatter.2.cloned.1.call-done = bf16[96,512]{1,0:T(8,128)(2,1)} async-done(((bf16[768,512]{1,0:T(8,128)(2,1)}), bf16[96,512]{1,0:T(8,128)(2,1)}) %reduce-scatter.2.cloned.1.call-update) | async-done | bytes 98320 | tf_op jit(solution)/shard_map/reduce_scatter | solution.py:37
  59.9 0.0 copy-done.3
  59.9 0.0 copy-start.2
  59.9 1.3 convert_reduce_fusion
  61.2 0.0 copy-done
  61.2 0.0 copy-done.2
  61.2 1.5 fusion.19
  62.7 0.0 copy-start.4
  62.8 0.0 all-reduce.2.cloned.1.call-update
  62.8 38.2 %psum.15 = f32[512]{0:T(512)S(1)} all-reduce(f32[512]{0:T(512)S(1)} %get-tuple-element.110), channel_id=1, replica_groups=mesh['node'=8,'edge'=4] {'node','edge'}, use_global_device_ids=true, to_apply=%region_5.6 | all-reduce | flops 512 | bytes 4096 | tf_op jit(solution)/shard_map/psum | solution.py:56
  100.9 0.0 copy-done.4
  101.0 0.3 fusion.32
  101.2 0.2 convolution_bitcast_fusion.1
  101.4 0.0 copy-start.5
  101.4 92.8 %all-reduce.2.cloned.1.call-done = f32[512,512]{1,0:T(8,128)} async-done(((f32[512,512]{1,0:T(8,128)}), f32[512,512]{1,0:T(8,128)}) %all-reduce.2.cloned.1.call-update) | async-done | bytes 1048592 | tf_op jit(solution)/shard_map/psum | solution.py:56
  194.2 1.8 fusion.17
  196.0 0.0 copy-done.5
  196.0 0.9 fusion.18
  (3 shorter events, 0.0 us)
Async XLA Ops:
  6.5 54.7 %copy-start = (bf16[512,512]{1,0:T(8,128)(2,1)S(1)}, bf16[512,512]{1,0:T(8,128)(2,1)}, u32[]{:S(2)}) copy-start(bf16[512,512]{1,0:T(8,128)(2,1)} %param.16) | copy-start | bytes 1572868
  6.5 53.3 %reduce-scatter.2.cloned.1.call-start = ((), (), s32[]{:S(2)}) async-start(), calls=%async_computation.1 | async-start | bytes 884736 | tf_op jit(solution)/shard_map/reduce_scatter | solution.py:37
  26.7 0.9 copy-start.1
  26.7 33.2 %copy-start.3 = (bf16[512,512]{1,0:T(8,128)(2,1)S(1)}, bf16[512,512]{1,0:T(8,128)(2,1)}, u32[]{:S(2)}) copy-start(bf16[512,512]{1,0:T(8,128)(2,1)} %param.15) | copy-start | bytes 1572868
  26.7 0.9 copy-start.6
  27.6 166.6 %all-reduce.2.cloned.1.call-start = ((), (), s32[]{:S(2)}) async-start(), calls=%async_computation.2 | async-start | bytes 2097152 | tf_op jit(solution)/shard_map/psum | solution.py:56
  59.9 1.3 copy-start.2
  62.7 38.2 %copy-start.4 = (bf16[512,512]{1,0:T(8,128)(2,1)S(1)}, bf16[512,512]{1,0:T(8,128)(2,1)}, u32[]{:S(2)}) copy-start(bf16[512,512]{1,0:T(8,128)(2,1)} %param.14) | copy-start | bytes 1572868
  101.4 94.6 %copy-start.5 = (bf16[512,512]{1,0:T(8,128)(2,1)S(1)}, bf16[512,512]{1,0:T(8,128)(2,1)}, u32[]{:S(2)}) copy-start(bf16[512,512]{1,0:T(8,128)(2,1)} %param.17) | copy-start | bytes 1572868
Sparse Core Ops, SparseCore 0:
  27.7 32.1 reduce-scatter.1
  65.1 129.1 all-reduce.1
where the time goes:
time: 204 us
  waiting for transfers between devices  125 us (61%)
  blocking collectives  50.2 us (25%)
  between operations  13.5 us (7%)
  matrix products  7.58 us (4%)
  local copies, waits for them, and re-layouts  5.46 us (3%)
    psum x1, waiting for transfers between devices, body(): gram_whole, key_whole = lax.psum((gram_local, key_local), ('node', 'edge'))  92.8 us
    psum x1, blocking collectives, body(): gram_whole, key_whole = lax.psum((gram_local, key_local), ('node', 'edge'))  38.2 us
    reduce_scatter x1, waiting for transfers between devices, body(): lax.psum_scatter(stacked.reshape(lax.axis_size('node') * owned, width).as...  32.2 us
    all_gather x1, blocking collectives, body(): gathered = lax.all_gather(node_feats, 'edge', axis=0, tiled=True)  12 us
  transfers between devices with their start and end apart: 2, of which 2 were waited for; matrix products, arithmetic and copies ran while one was open for 0% of the time, Pallas kernels for 0%

commit v1 on v0

--- a/solution.py
+++ b/solution.py
@@ -53,7 +53,7 @@
     )
     key_local = jnp.sum(key_feats.astype(jnp.float32), axis=0)
     query_wide = query_feats.astype(jnp.float32)
-    gram_whole, key_whole = lax.psum((gram_local, key_local), ("node", "edge"))
+    gram_whole, key_whole = lax.psum(lax.psum((gram_local, key_local), "edge"), "node")
     numer = jnp.dot(query_wide, gram_whole, precision=lax.Precision.HIGHEST)
     denom = jnp.dot(query_wide, key_whole, precision=lax.Precision.HIGHEST)
     attended = (numer / denom[:, None]).astype(jnp.bfloat16)

time: 204 us -> 185 us (0.907)
  blocking collectives: 50.2 us -> 35.4 us
  waiting for transfers between devices: 125 us -> 121 us
    psum x1 -> x2, blocking collectives: 38.2 us -> 23.5 us  [the longest x1 14.4 us: body(): lax.psum(lax.psum((gram_local, key_local), 'edge'), 'node')]
    psum x1 -> x2, waiting for transfers between devices: 92.8 us -> 88.7 us  [the longest x1 50.9 us: body(): lax.psum((gram_local, key_local), 'edge')]
  transfers between devices with their start and end apart: 2 -> 3, of which waited for: 2 -> 3; matrix products, arithmetic and copies ran while one was open for 0% -> 0% of each run, Pallas kernels for 0% -> 0%
where the time goes in v1:
time: 185 us
  waiting for transfers between devices  121 us (65%)
  blocking collectives  35.4 us (19%)
  between operations  13.2 us (7%)
  matrix products  7.59 us (4%)
  local copies, waits for them, and re-layouts  5.51 us (3%)
  loops' own time  2 us (1%)
    psum x1, waiting for transfers between devices, body(): lax.psum((gram_local, key_local), 'edge')  50.9 us
    psum x1, waiting for transfers between devices, body(): lax.psum(lax.psum((gram_local, key_local), 'edge'), 'node')  37.8 us
    reduce_scatter x1, waiting for transfers between devices, body(): lax.psum_scatter(stacked.reshape(lax.axis_size('node') * owned, width).as...  32.2 us
    psum x1, blocking collectives, body(): lax.psum(lax.psum((gram_local, key_local), 'edge'), 'node')  14.4 us
    all_gather x1, blocking collectives, body(): gathered = lax.all_gather(node_feats, 'edge', axis=0, tiled=True)  12 us
    psum x1, blocking collectives, body(): lax.psum((gram_local, key_local), 'edge')  9.07 us
  transfers between devices with their start and end apart: 3, of which 3 were waited for; matrix products, arithmetic and copies ran while one was open for 0% of the time, Pallas kernels for 0%

profile of v1, /device:TPU:0, one launch (start us, length us, event | category | flops | bytes accessed | tf_op | source)
XLA Modules:
  0.0 184.7 jit_solution(4290078687317774802)
XLA Ops:
  6.5 0.0 copy-start
  6.5 0.0 reduce-scatter.2.cloned.1.call-start
  6.5 12.0 %all_gather.3 = bf16[512,512]{1,0:T(8,128)(2,1)S(1)} all-gather(bf16[128,512]{1,0:T(8,128)(2,1)} %param.10), channel_id=1, replica_groups=mesh['node'=8,'edge'=4] {'edge'}, dimensions={0}, use_global_device_ids=true | all-gather | bytes 655360 | tf_op jit(solution)/shard_map/all_gather | solution.py:13
  18.5 8.2 %while.12 = (s32[]{:T(128)}, bf16[3,256,512]{2,1,0:T(8,128)(2,1)S(1)}, s32[3]{0:T(128)S(1)}, s32[4,768]{1,0:T(4,128)}, s32[4,768]{1,0:T(4,128)}, /*index=5*/bf16...) while((s32[]{:T(128)}, ...), condition=%wide.region_1.2_spmd.clone.clone, body=%wide.region_0.1_spmd.clone.clone.sunk | while | flops 136839168 | bytes 1073399 | solution.py:36
  18.5 0.6 dynamic_slice.17
  19.8 0.9 constant_dynamic-slice_fusion.3
  20.7 0.5 fusion.46
  21.3 0.6 dynamic_slice.17
  22.5 0.9 constant_dynamic-slice_fusion.3
  23.5 0.5 fusion.46
  24.0 0.6 dynamic_slice.17
  25.3 0.9 constant_dynamic-slice_fusion.3
  26.2 0.5 fusion.46
  26.8 0.0 copy-start.1
  26.8 0.0 copy-start.3
  26.8 0.0 copy-start.6
  26.8 0.8 copy-done.1
  27.7 0.0 reduce-scatter.2.cloned.1.call-update
  27.7 0.0 all-reduce.3.cloned.1.call-start
  27.7 0.0 copy-done.6
  27.8 32.2 %reduce-scatter.2.cloned.1.call-done = bf16[96,512]{1,0:T(8,128)(2,1)} async-done(((bf16[768,512]{1,0:T(8,128)(2,1)}), bf16[96,512]{1,0:T(8,128)(2,1)}) %reduce-scatter.2.cloned.1.call-update) | async-done | bytes 98320 | tf_op jit(solution)/shard_map/reduce_scatter | solution.py:37
  60.0 0.0 copy-done.3
  60.0 0.0 copy-start.2
  60.0 1.3 convert_reduce_fusion
  61.3 0.0 copy-done
  61.3 0.0 copy-done.2
  61.3 1.6 fusion.19
  62.9 0.0 all-reduce.3.cloned.1.call-update
  62.9 0.0 all-reduce.5.cloned.1.call-start
  62.9 50.9 %all-reduce.3.cloned.1.call-done = f32[512,512]{1,0:T(8,128)} async-done(((f32[512,512]{1,0:T(8,128)}), f32[512,512]{1,0:T(8,128)}) %all-reduce.3.cloned.1.call-update) | async-done | bytes 1048592 | tf_op jit(solution)/shard_map/psum | solution.py:56
  113.8 0.0 copy-start.4
  113.8 0.0 all-reduce.5.cloned.1.call-update
  113.9 9.1 %psum.30 = f32[512]{0:T(512)S(1)} all-reduce(f32[512]{0:T(512)S(1)} %get-tuple-element.110), channel_id=1, replica_groups=mesh['node'=8,'edge'=4] {'edge'}, use_global_device_ids=true, to_apply=%region_6.7 | all-reduce | flops 512 | bytes 4096 | tf_op jit(solution)/shard_map/psum | solution.py:56
  122.9 14.4 %psum.31 = f32[512]{0:T(512)S(1)} all-reduce(f32[512]{0:T(512)S(1)} %psum.30), channel_id=1, replica_groups=mesh['node'=8,'edge'=4] {'node'}, use_global_device_ids=true, to_apply=%region_7.8 | all-reduce | flops 512 | bytes 4096 | tf_op jit(solution)/shard_map/psum | solution.py:56
  137.3 0.0 copy-done.4
  137.3 0.3 fusion.32
  137.6 0.2 convolution_bitcast_fusion.1
  137.8 0.0 copy-start.5
  137.8 37.8 %all-reduce.5.cloned.1.call-done = f32[512,512]{1,0:T(8,128)} async-done(((f32[512,512]{1,0:T(8,128)}), f32[512,512]{1,0:T(8,128)}) %all-reduce.5.cloned.1.call-update) | async-done | bytes 1048592 | tf_op jit(solution)/shard_map/psum | solution.py:56
  175.5 1.8 fusion.17
  177.3 0.0 copy-done.5
  177.3 0.9 fusion.18
  (3 shorter events, 0.0 us)
Async XLA Ops:
  6.5 54.7 %copy-start = (bf16[512,512]{1,0:T(8,128)(2,1)S(1)}, bf16[512,512]{1,0:T(8,128)(2,1)}, u32[]{:S(2)}) copy-start(bf16[512,512]{1,0:T(8,128)(2,1)} %param.16) | copy-start | bytes 1572868
  6.5 53.4 %reduce-scatter.2.cloned.1.call-start = ((), (), s32[]{:S(2)}) async-start(), calls=%async_computation.1 | async-start | bytes 884736 | tf_op jit(solution)/shard_map/reduce_scatter | solution.py:37
  26.8 0.9 copy-start.1
  26.8 33.2 %copy-start.3 = (bf16[512,512]{1,0:T(8,128)(2,1)S(1)}, bf16[512,512]{1,0:T(8,128)(2,1)}, u32[]{:S(2)}) copy-start(bf16[512,512]{1,0:T(8,128)(2,1)} %param.15) | copy-start | bytes 1572868
  26.8 0.9 copy-start.6
  27.7 86.2 %all-reduce.3.cloned.1.call-start = ((), (), s32[]{:S(2)}) async-start(), calls=%async_computation.2 | async-start | bytes 2097152 | tf_op jit(solution)/shard_map/psum | solution.py:56
  60.0 1.3 copy-start.2
  62.9 112.7 %all-reduce.5.cloned.1.call-start = ((), (), s32[]{:S(2)}) async-start(), calls=%async_computation.3 | async-start | bytes 2097152 | tf_op jit(solution)/shard_map/psum | solution.py:56
  113.8 23.5 %copy-start.4 = (bf16[512,512]{1,0:T(8,128)(2,1)S(1)}, bf16[512,512]{1,0:T(8,128)(2,1)}, u32[]{:S(2)}) copy-start(bf16[512,512]{1,0:T(8,128)(2,1)} %param.14) | copy-start | bytes 1572868
  137.8 39.6 %copy-start.5 = (bf16[512,512]{1,0:T(8,128)(2,1)S(1)}, bf16[512,512]{1,0:T(8,128)(2,1)}, u32[]{:S(2)}) copy-start(bf16[512,512]{1,0:T(8,128)(2,1)} %param.17) | copy-start | bytes 1572868
Sparse Core Ops, SparseCore 0:
  27.8 32.1 reduce-scatter.1
  63.0 50.7 all-reduce.2
  116.2 59.2 all-reduce.4
